TPU v7x, 32 devices: a whole 2x2x4 slice. The times are simulated.
32 devices in a mesh: pix: 4 (over x, core), scan: 8 (over z, y).
Axes of the slice: x: 2, y: 2, z: 4, core: 2. Of those that a mesh axis runs over, the one named last changes fastest.
Arguments:
- scan_data: bfloat16 [128, 512, 512], P('pix', 'scan'), may hold values from -6 to 6
- pixel_coords: int32 [2, 128], P(None, 'pix'), may hold values from -6 to 6, as said below
- aberrations: float32 [4], replicated, may hold values from -3 to 3
Outputs:
- object_wave: float32 [2, 512, 512], P(None, 'scan', 'pix')
Inputs may be any that keep to these rules, and one draw needn't show every extreme that they name: `pixel_coords`: each column is a distinct pair (u, v) of integers with u * u + v * v <= 40; their order is arbitrary.
All inputs are finite; a program needn't handle non-finite values.
Results may differ from a plain program's by a relative error of at most 0.0043.
Values may be sent and summed in bfloat16 or wider, within the bound.
A program may use at most 64 MiB of HBM per device.

v0:
```python
import functools
import math

import jax
import jax.numpy as jnp
import numpy as np
from jax import lax
from jax.experimental import pallas as pl
from jax.experimental.pallas import tpu as pltpu
from jax.sharding import PartitionSpec as P

STEP = 8
EXTENT = 6
REACH = STEP * EXTENT
APERTURE = 40 * STEP * STEP


def centred(length):
    return np.arange(length // 2) - length // 4


def table_pair(freqs, places, length):
    angles = (np.outer(freqs, places) % length) * (2.0 * math.pi / length)
    return np.cos(angles), np.sin(angles)


def aberration(px, py, a):
    px = px.astype(jnp.float32)
    py = py.astype(jnp.float32)
    radial = (px * px + py * py) / float(APERTURE)
    return (
        a[0] * radial
        + a[1] * (px * px - py * py) / float(APERTURE)
        + a[2] * 2.0 * px * py / float(APERTURE)
        + a[3] * radial * radial
    )


def partial_kernel(
    group, rows, coords, aber, data, forward, columns, out, base_re, base_im, tab_re, tab_im, spec
):
    step = pl.program_id(0)
    band_x = out.shape[1]
    band_y = out.shape[2]
    shifts = tab_re.shape[0]
    coeffs = [aber[i] for i in range(4)]

    @pl.when(step == 0)
    def _():
        out[...] = jnp.zeros_like(out)
        tall, wide = base_re.shape
        chunk = 16

        @pl.loop(0, tall // chunk)
        def _(i):
            at = pl.ds(pl.multiple_of(i * chunk, chunk), chunk)
            px = lax.broadcasted_iota(jnp.int32, (chunk, wide), 0) + (
                i * chunk - band_x // 2 - REACH
            )
            py = lax.broadcasted_iota(jnp.int32, (chunk, wide), 1) - (band_y // 2 + REACH)
            inside = px * px + py * py <= APERTURE
            phase = aberration(px, py, coeffs)
            real = jnp.cos(phase)
            real = jnp.where(real == 0.0, 1e-12, real)
            base_re[at, :] = jnp.where(inside, real, 0.0)
            base_im[at, :] = jnp.where(inside, jnp.sin(phase), 0.0)
            for s in range(shifts):
                tab_re[s, at, :] = base_re[at, STEP * s : STEP * s + band_y]
                tab_im[s, at, :] = base_im[at, STEP * s : STEP * s + band_y]

    me = lax.axis_index("scan")
    table = columns[me]
    rowspec = jnp.dot(data[...], forward[...], preferred_element_type=jnp.float32)

    def transform(g):
        mine = rowspec[g * rows : (g + 1) * rows].astype(jnp.bfloat16)
        turned = jnp.concatenate([mine[:, band_y:], -mine[:, :band_y]], axis=1)
        if rows % 16 == 0:
            both = jnp.concatenate([mine, turned], axis=0)
            spec[g] = jnp.dot(table, both, preferred_element_type=jnp.float32)
        else:
            spec[g] = jnp.dot(
                table[:, :rows], mine, preferred_element_type=jnp.float32
            ) + jnp.dot(table[:, rows:], turned, preferred_element_type=jnp.float32)

    def weigh(g):
        pixel = step * group + g
        u = coords[0, pixel]
        v = coords[1, pixel]
        kx = jnp.full((8, 128), STEP * u, jnp.int32)
        ky = jnp.full((8, 128), STEP * v, jnp.int32)
        own = aberration(kx, ky, coeffs)
        cos_own = jnp.concatenate([jnp.cos(own)] * (band_y // 128), axis=1)
        sin_own = jnp.concatenate([jnp.sin(own)] * (band_y // 128), axis=1)
        for r in range(0, band_x, 8):
            left = pl.ds(pl.multiple_of(r + REACH - STEP * u, 8), 8)
            right = pl.ds(pl.multiple_of(r + REACH + STEP * u, 8), 8)
            ar = tab_re[EXTENT - v, left, :]
            ai = tab_im[EXTENT - v, left, :]
            br = tab_re[EXTENT + v, right, :]
            bi = tab_im[EXTENT + v, right, :]
            both = ar * br != 0.0
            wr = cos_own * (ar - br) + sin_own * (ai - bi)
            wi = cos_own * (ai + bi) - sin_own * (ar + br)
            wr = jnp.where(both, 0.0, wr)
            wi = jnp.where(both, 0.0, wi)
            sr = spec[g, r : r + 8, :band_y]
            si = spec[g, r : r + 8, band_y:]
            out[0, r : r + 8, :] += sr * wr - si * wi
            out[1, r : r + 8, :] += sr * wi + si * wr

    transform(0)
    for g in range(group):
        if g + 1 < group:
            transform(g + 1)
        weigh(g)


def partial_spectrum(scan_data, pixel_coords, aberrations, scan_count):
    pixels, rows, breadth = scan_data.shape
    height = rows * scan_count
    band_x, band_y = height // 2, breadth // 2
    group = 4
    fc, fs = table_pair(centred(breadth), np.arange(breadth), breadth)
    forward = jnp.asarray(np.concatenate([fc.T, -fs.T], axis=1), jnp.bfloat16)
    cc, cs = table_pair(centred(height), np.arange(height), height)
    stacked = np.stack(
        [
            np.concatenate([cc[:, i : i + rows], cs[:, i : i + rows]], axis=1)
            for i in range(0, height, rows)
        ]
    )
    columns = jnp.asarray(stacked, jnp.bfloat16)
    tall = band_x + 2 * REACH
    wide = -(-(band_y + 2 * REACH) // 128) * 128
    whole = lambda shape: pl.BlockSpec(shape, lambda i: (0,) * len(shape))
    shifts = 2 * EXTENT + 1
    return pl.pallas_call(
        functools.partial(partial_kernel, group, rows),
        grid=(pixels // group,),
        out_shape=jax.ShapeDtypeStruct((2, band_x, band_y), jnp.float32),
        in_specs=[
            pl.BlockSpec(memory_space=pltpu.SMEM),
            pl.BlockSpec(memory_space=pltpu.SMEM),
            pl.BlockSpec((group * rows, breadth), lambda i: (i, 0)),
            whole(forward.shape),
            whole(columns.shape),
        ],
        out_specs=whole((2, band_x, band_y)),
        scratch_shapes=[
            pltpu.VMEM((tall, wide), jnp.float32),
            pltpu.VMEM((tall, wide), jnp.float32),
            pltpu.VMEM((shifts, tall, band_y), jnp.float32),
            pltpu.VMEM((shifts, tall, band_y), jnp.float32),
            pltpu.VMEM((group, band_x, 2 * band_y), jnp.float32),
        ],
        compiler_params=pltpu.CompilerParams(vmem_limit_bytes=60 * 1024 * 1024),
        name="partial_spectrum",
    )(pixel_coords, aberrations, scan_data.reshape(pixels * rows, breadth), forward, columns)


def on_device(scan_data, pixel_coords, aberrations):
    highest = lax.Precision.HIGHEST
    pixels, rows, breadth = scan_data.shape
    scan_count = lax.axis_size("scan")
    pix_count = lax.axis_size("pix")
    height = rows * scan_count
    partial = partial_spectrum(scan_data, pixel_coords, aberrations, scan_count)
    total = lax.psum(partial, ("pix", "scan"))
    share = breadth // pix_count
    ic, isn = table_pair(centred(height), np.arange(height), height)
    inverse_x = jnp.asarray(np.stack([ic, isn]), jnp.float32)
    inverse_x = lax.dynamic_slice_in_dim(inverse_x, lax.axis_index("scan") * rows, rows, 2)
    jc, js = table_pair(centred(breadth), np.arange(breadth), breadth)
    inverse_y = jnp.asarray(np.stack([jc, js]), jnp.float32)
    inverse_y = lax.dynamic_slice_in_dim(inverse_y, lax.axis_index("pix") * share, share, 2)
    dot = functools.partial(jnp.einsum, precision=highest)
    left = dot("tkx,pkq->tpxq", inverse_x, total)
    mid_re = left[0, 0] - left[1, 1]
    mid_im = left[1, 0] + left[0, 1]
    mid = jnp.stack([mid_re, mid_im])
    right = dot("pxq,tqy->tpxy", mid, inverse_y)
    result = jnp.stack([right[0, 0] - right[1, 1], right[1, 0] + right[0, 1]])
    return result * (1.0 / (height * breadth))


def solution(mesh):
    placed = (P("pix", "scan", None), P(None, "pix"), P())
    return jax.shard_map(
        on_device, mesh=mesh, in_specs=placed, out_specs=P(None, "scan", "pix"), check_vma=False
    )
```

profile of v0, /device:TPU:0, one launch (start us, length us, event | category | flops | bytes accessed | tf_op | source)
XLA Modules:
  0.0 169.0 jit_solution(5474937767979363411)
XLA Ops:
  6.5 0.0 all-reduce.2.cloned.1.call-start
  6.5 20.0 %partial_spectrum.1 = f32[2,256,256]{2,1,0:T(8,128)} custom-call(s32[2,32]{1,0:T(2,128)} %coords.1, f32[4]{0:T(128)} %aber.1, bf16[2048,512]{1,0:T(8,128)(2,1)} %bitcast.39, bf16[512,512]{1,0:T(8,128)(2,1)} %constant.24.clone.forward, bf16[8,256,128]{2,1,0:T(8,128)(2,1)} %constant.25.clone.columns), custom_call_target="tpu_custom_call" | custom-call | tf_op jit(solution)/shard_map/partial_spectrum/pallas_call | solution.py:138
  26.6 0.0 all-reduce.2.cloned.1.call-update
  26.6 131.9 %all-reduce.2.cloned.1.call-done = f32[2,256,256]{2,1,0:T(8,128)} async-done(((f32[2,256,256]{2,1,0:T(8,128)}), f32[2,256,256]{2,1,0:T(8,128)}) %all-reduce.2.cloned.1.call-update) | async-done | bytes 524304 | tf_op jit(solution)/shard_map/psum | solution.py:169
  158.6 1.5 convolution_bitcast_fusion
  160.1 1.4 convolution_bitcast_fusion.1
  161.5 0.6 maximum_multiply_fusion
  (3 shorter events, 0.0 us)
Async XLA Ops:
  6.5 152.0 %all-reduce.2.cloned.1.call-start = ((), (), s32[]{:S(2)}) async-start(), calls=%async_computation | async-start | bytes 1048576 | tf_op jit(solution)/shard_map/psum | solution.py:169
Sparse Core Ops, SparseCore 0:
  26.7 131.7 all-reduce.1
where the time goes:
time: 169 us
  waiting for transfers between devices  132 us (78%)
  Pallas kernels  20 us (12%)
  between operations  13.4 us (8%)
  matrix products  2.87 us (2%)
    psum x1, waiting for transfers between devices, on_device(): total = lax.psum(partial, ('pix', 'scan'))  132 us
    pallas_call x1, Pallas kernels, partial_spectrum(): pl.pallas_call(functools.partial(partial_kernel, group, rows), grid=(pixe...  20 us
  transfers between devices with their start and end apart: 1, of which 1 were waited for; matrix products, arithmetic and copies ran while one was open for 0% of the time, Pallas kernels for 0%

commit v1 on v0

--- a/solution.py
+++ b/solution.py
@@ -37,11 +37,10 @@
 
 
 def partial_kernel(
-    group, rows, coords, aber, data, forward, columns, out, base_re, base_im, tab_re, tab_im, spec
+    group, rows, coords, aber, data, forward, columns, final, base_re, base_im, tab_re, tab_im, spec, out
 ):
     step = pl.program_id(0)
-    band_x = out.shape[1]
-    band_y = out.shape[2]
+    band_x, band_y = out.shape[1:]
     shifts = tab_re.shape[0]
     coeffs = [aber[i] for i in range(4)]
 
@@ -115,6 +114,95 @@
             transform(g + 1)
         weigh(g)
 
+    @pl.when(step == pl.num_programs(0) - 1)
+    def _():
+        final[...] = out[...].astype(final.dtype)
+
+
+def sum_kernel(count, width, part, total, arrived, own, send_a, take_a, send_b, take_b):
+    me = lax.axis_index("pix") * width + lax.axis_index("scan")
+
+    def place(k):
+        other = lax.rem(me + k, count)
+        return other, {"pix": other // width, "scan": lax.rem(other, width)}
+
+    barrier = pltpu.get_barrier_semaphore()
+
+    @pl.loop(1, count)
+    def _(k):
+        pl.semaphore_signal(
+            barrier, inc=1, device_id=place(k)[1], device_id_type=pl.DeviceIdType.MESH
+        )
+
+    pl.semaphore_wait(barrier, count - 1)
+
+    def scatter(k):
+        other, where = place(k)
+        return pltpu.make_async_remote_copy(
+            src_ref=part.at[other],
+            dst_ref=arrived.at[k],
+            send_sem=send_a.at[k],
+            recv_sem=take_a.at[k],
+            device_id=where,
+            device_id_type=pl.DeviceIdType.MESH,
+        )
+
+    def gather(k):
+        return pltpu.make_async_remote_copy(
+            src_ref=own,
+            dst_ref=total.at[me],
+            send_sem=send_b.at[k],
+            recv_sem=take_b.at[k],
+            device_id=place(k)[1],
+            device_id_type=pl.DeviceIdType.MESH,
+        )
+
+    @pl.loop(1, count)
+    def _(k):
+        scatter(k).start()
+
+    def add(k, summed):
+        scatter(k).wait_recv()
+        return summed + arrived[k].astype(jnp.float32)
+
+    summed = lax.fori_loop(1, count, add, part[me].astype(jnp.float32))
+    own[...] = summed.astype(own.dtype)
+    total[me] = own[...]
+
+    @pl.loop(1, count)
+    def _(k):
+        gather(k).start()
+
+    @pl.loop(1, count)
+    def _(k):
+        scatter(k).wait_send()
+        gather(k).wait()
+
+
+def sum_everywhere(partial):
+    width = lax.axis_size("scan")
+    count = lax.axis_size("pix") * width
+    parts, band_x, band_y = partial.shape
+    lines = parts * band_x // count
+    if parts * band_x % (16 * count):
+        return lax.psum(partial.astype(jnp.float32), ("pix", "scan"))
+    pieces = (count, lines, band_y)
+    vmem = pl.BlockSpec(memory_space=pltpu.VMEM)
+    total = pl.pallas_call(
+        functools.partial(sum_kernel, count, width),
+        out_shape=jax.ShapeDtypeStruct(pieces, partial.dtype),
+        in_specs=[vmem],
+        out_specs=vmem,
+        scratch_shapes=[
+            pltpu.VMEM(pieces, partial.dtype),
+            pltpu.VMEM(pieces[1:], partial.dtype),
+        ]
+        + [pltpu.SemaphoreType.DMA((count,))] * 4,
+        compiler_params=pltpu.CompilerParams(collective_id=0, has_side_effects=True),
+        name="sum_everywhere",
+    )(partial.reshape(pieces))
+    return total.reshape(partial.shape).astype(jnp.float32)
+
 
 def partial_spectrum(scan_data, pixel_coords, aberrations, scan_count):
     pixels, rows, breadth = scan_data.shape
@@ -138,7 +226,7 @@
     return pl.pallas_call(
         functools.partial(partial_kernel, group, rows),
         grid=(pixels // group,),
-        out_shape=jax.ShapeDtypeStruct((2, band_x, band_y), jnp.float32),
+        out_shape=jax.ShapeDtypeStruct((2, band_x, band_y), jnp.bfloat16),
         in_specs=[
             pl.BlockSpec(memory_space=pltpu.SMEM),
             pl.BlockSpec(memory_space=pltpu.SMEM),
@@ -153,6 +241,7 @@
             pltpu.VMEM((shifts, tall, band_y), jnp.float32),
             pltpu.VMEM((shifts, tall, band_y), jnp.float32),
             pltpu.VMEM((group, band_x, 2 * band_y), jnp.float32),
+            pltpu.VMEM((2, band_x, band_y), jnp.float32),
         ],
         compiler_params=pltpu.CompilerParams(vmem_limit_bytes=60 * 1024 * 1024),
         name="partial_spectrum",
@@ -166,7 +255,7 @@
     pix_count = lax.axis_size("pix")
     height = rows * scan_count
     partial = partial_spectrum(scan_data, pixel_coords, aberrations, scan_count)
-    total = lax.psum(partial, ("pix", "scan"))
+    total = sum_everywhere(partial)
     share = breadth // pix_count
     ic, isn = table_pair(centred(height), np.arange(height), height)
     inverse_x = jnp.asarray(np.stack([ic, isn]), jnp.float32)

time: 169 us -> 48.8 us (0.29)
  waiting for transfers between devices: 132 us -> 0 us
  Pallas kernels: 20 us -> 45.2 us
  between operations: 13.4 us -> 0.05 us
    psum x1 -> x0, waiting for transfers between devices: 132 us -> none  [on_device(): total = lax.psum(partial, ('pix', 'scan'))]
    pallas_call x0 -> x1, Pallas kernels: none -> 25.1 us  [sum_everywhere(): pl.pallas_call(functools.partial(sum_kernel, count, width), out_shape=jax...]
  transfers between devices with their start and end apart: 1 -> 0, of which waited for: 1 -> 0; matrix products, arithmetic and copies ran while one was open for 0% -> 0% of each run, Pallas kernels for 0% -> 0%
where the time goes in v1:
time: 48.8 us; the launch traced here: 48.5 us
  Pallas kernels  45.2 us (93%)
  matrix products  2.63 us (5%)
  other arithmetic  0.67 us (1%)
    pallas_call x1, Pallas kernels, sum_everywhere(): pl.pallas_call(functools.partial(sum_kernel, count, width), out_shape=jax...  25.1 us
    pallas_call x1, Pallas kernels, partial_spectrum(): pl.pallas_call(functools.partial(partial_kernel, group, rows), grid=(pixe...  20 us
    dot_general x1, matrix products, on_device(): right = dot('pxq,tqy->tpxy', mid, inverse_y)  1.36 us
    dot_general x1, matrix products, on_device(): left = dot('tkx,pkq->tpxq', inverse_x, total)  1.27 us

profile of v1, /device:TPU:0, one launch (start us, length us, event | category | flops | bytes accessed | tf_op | source)
XLA Modules:
  0.0 48.5 jit_solution(7310142373269561877)
XLA Ops:
  0.0 20.0 %partial_spectrum.1 = bf16[2,256,256]{2,1,0:T(8,128)(2,1)} custom-call(s32[2,32]{1,0:T(2,128)} %coords.1, f32[4]{0:T(128)} %aber.1, bf16[2048,512]{1,0:T(8,128)(2,1)} %bitcast.41, bf16[512,512]{1,0:T(8,128)(2,1)} %constant.24.clone.forward, bf16[8,256,128]{2,1,0:T(8,128)(2,1)} %constant.25.clone.columns), custom_call_target="tpu_custom_call" | custom-call | tf_op jit(solution)/shard_map/partial_spectrum/pallas_call | solution.py:226
  20.0 25.1 %sum_everywhere.1 = bf16[32,16,256]{2,1,0:T(8,128)(2,1)} custom-call(bf16[32,16,256]{2,1,0:T(8,128)(2,1)} %bitcast.43), custom_call_target="tpu_custom_call" | custom-call | tf_op jit(solution)/shard_map/sum_everywhere/pallas_call | solution.py:191
  45.2 1.3 %convolution_bitcast_fusion = f32[2,2,64,256]{3,2,0,1:T(8,128)S(1)} fusion(bf16[2,256,256,1]{2,1,3,0:T(8,128)(2,1)} %bitcast.42, f32[2,256,512]{1,2,0:T(8,128)} %constant.26.clone, s32[]{:T(128)S(6)} %select_n.7), kind=kOutput, calls=%fused_computation | convolution fusion | flops 201326592 | bytes 655364 | tf_op jit(solution)/shard_map/tkx,pkq->tpxq/dot_general | solution.py:267
  46.5 1.4 %convolution_bitcast_fusion.1 = f32[2,2,64,128]{3,2,1,0:T(8,128)S(1)} fusion(f32[2,256,512]{1,2,0:T(8,128)} %constant.26.clone, s32[]{:T(128)S(6)} %select_n.6, f32[1,64,256]{2,1,0:T(8,128)S(1)} %fusion.6, f32[1,64,256]{2,1,0:T(8,128)S(1)} %fusion.8), kind=kOutput, calls=%fused_computation.1 | convolution fusion | flops 100696064 | bytes 524292 | tf_op jit(solution)/shard_map/pxq,tqy->tpxy/dot_general | solution.py:271
  47.9 0.6 %maximum_multiply_fusion = f32[2,64,128]{2,1,0:T(8,128)} fusion(f32[1,64,128]{2,1,0:T(8,128)S(1)} %get-tuple-element.6, f32[1,64,128]{2,1,0:T(8,128)S(1)} %get-tuple-element.5), kind=kLoop, calls=%fused_computation.15 | loop fusion | flops 32768 | bytes 131072 | tf_op jit(solution)/shard_map/mul | solution.py:273
  (3 shorter events, 0.0 us)

commit v2 on v0

--- a/solution.py
+++ b/solution.py
@@ -37,11 +37,10 @@
 
 
 def partial_kernel(
-    group, rows, coords, aber, data, forward, columns, out, base_re, base_im, tab_re, tab_im, spec
+    group, rows, coords, aber, data, forward, columns, final, base_re, base_im, tab_re, tab_im, spec, out
 ):
     step = pl.program_id(0)
-    band_x = out.shape[1]
-    band_y = out.shape[2]
+    band_x, band_y = out.shape[1:]
     shifts = tab_re.shape[0]
     coeffs = [aber[i] for i in range(4)]
 
@@ -114,6 +113,114 @@
         if g + 1 < group:
             transform(g + 1)
         weigh(g)
+
+    @pl.when(step == pl.num_programs(0) - 1)
+    def _():
+        final[...] = out[...].astype(final.dtype)
+
+
+def sum_kernel(across, along, part, total, arrived, held, crossed, own, block, *sems):
+    scan_me = lax.axis_index("scan")
+    pix_me = lax.axis_index("pix")
+
+    def peer(axis, k):
+        if axis == "scan":
+            return lax.rem(scan_me + k, along)
+        return lax.rem(pix_me + k, across)
+
+    def copy(axis, k, source, target, stage):
+        return pltpu.make_async_remote_copy(
+            src_ref=source,
+            dst_ref=target,
+            send_sem=sems[2 * stage].at[k],
+            recv_sem=sems[2 * stage + 1].at[k],
+            device_id={axis: peer(axis, k)},
+            device_id_type=pl.DeviceIdType.MESH,
+        )
+
+    barrier = pltpu.get_barrier_semaphore()
+    for axis, count in (("scan", along), ("pix", across)):
+        for k in range(1, count):
+            pl.semaphore_signal(
+                barrier,
+                inc=1,
+                device_id={axis: peer(axis, k)},
+                device_id_type=pl.DeviceIdType.MESH,
+            )
+    pl.semaphore_wait(barrier, along + across - 2)
+
+    pending = [
+        copy("scan", k, part.at[peer("scan", k)], arrived.at[k], 0) for k in range(1, along)
+    ]
+    for c in pending:
+        c.start()
+    for c in pending:
+        c.wait_recv()
+    lines = own.shape[0]
+    for j in range(across):
+        rows = pl.ds(j * lines, lines)
+        summed = part[scan_me, rows, :].astype(jnp.float32)
+        for k in range(1, along):
+            summed += arrived[k, rows, :].astype(jnp.float32)
+        held[j] = summed.astype(held.dtype)
+
+    second = [
+        copy("pix", k, held.at[peer("pix", k)], crossed.at[k], 1) for k in range(1, across)
+    ]
+    for c in second:
+        c.start()
+    for c in second:
+        c.wait_recv()
+    summed = held[pix_me].astype(jnp.float32)
+    for k in range(1, across):
+        summed += crossed[k].astype(jnp.float32)
+    own[...] = summed.astype(own.dtype)
+    block[pix_me] = own[...]
+
+    third = [copy("pix", k, own, block.at[pix_me], 2) for k in range(1, across)]
+    for c in third:
+        c.start()
+    for c in third:
+        c.wait_recv()
+
+    fourth = [copy("scan", k, block, total.at[scan_me], 3) for k in range(1, along)]
+    for c in fourth:
+        c.start()
+    total[scan_me] = block[...]
+    for c in fourth:
+        c.wait_recv()
+    for c in pending + second + third + fourth:
+        c.wait_send()
+
+
+def sum_everywhere(partial):
+    along = lax.axis_size("scan")
+    across = lax.axis_size("pix")
+    parts, band_x, band_y = partial.shape
+    lines = parts * band_x // (along * across)
+    if parts * band_x % (16 * along * across):
+        return lax.psum(partial.astype(jnp.float32), ("pix", "scan"))
+    narrow = jnp.bfloat16
+    pieces = (along, across * lines, band_y)
+    vmem = pl.BlockSpec(memory_space=pltpu.VMEM)
+    total = pl.pallas_call(
+        functools.partial(sum_kernel, across, along),
+        out_shape=jax.ShapeDtypeStruct((along, across, lines, band_y), narrow),
+        in_specs=[vmem],
+        out_specs=vmem,
+        scratch_shapes=[
+            pltpu.VMEM(pieces, partial.dtype),
+            pltpu.VMEM((across, lines, band_y), narrow),
+            pltpu.VMEM((across, lines, band_y), narrow),
+            pltpu.VMEM((lines, band_y), narrow),
+            pltpu.VMEM((across, lines, band_y), narrow),
+        ]
+        + [pltpu.SemaphoreType.DMA((c,)) for c in (along, along, across, across)]
+        + [pltpu.SemaphoreType.DMA((c,)) for c in (across, across, along, along)],
+        compiler_params=pltpu.CompilerParams(collective_id=0, has_side_effects=True),
+        name="sum_everywhere",
+    )(partial.reshape(pieces))
+    return total.reshape(partial.shape).astype(jnp.float32)
 
 
 def partial_spectrum(scan_data, pixel_coords, aberrations, scan_count):
@@ -153,6 +260,7 @@
             pltpu.VMEM((shifts, tall, band_y), jnp.float32),
             pltpu.VMEM((shifts, tall, band_y), jnp.float32),
             pltpu.VMEM((group, band_x, 2 * band_y), jnp.float32),
+            pltpu.VMEM((2, band_x, band_y), jnp.float32),
         ],
         compiler_params=pltpu.CompilerParams(vmem_limit_bytes=60 * 1024 * 1024),
         name="partial_spectrum",
@@ -166,7 +274,7 @@
     pix_count = lax.axis_size("pix")
     height = rows * scan_count
     partial = partial_spectrum(scan_data, pixel_coords, aberrations, scan_count)
-    total = lax.psum(partial, ("pix", "scan"))
+    total = sum_everywhere(partial)
     share = breadth // pix_count
     ic, isn = table_pair(centred(height), np.arange(height), height)
     inverse_x = jnp.asarray(np.stack([ic, isn]), jnp.float32)

time: 169 us -> 55.1 us (0.33)
  waiting for transfers between devices: 132 us -> 0 us
  Pallas kernels: 20 us -> 51.5 us
  between operations: 13.4 us -> 0.05 us
    psum x1 -> x0, waiting for transfers between devices: 132 us -> none  [on_device(): total = lax.psum(partial, ('pix', 'scan'))]
    pallas_call x0 -> x1, Pallas kernels: none -> 31.4 us  [sum_everywhere(): pl.pallas_call(functools.partial(sum_kernel, across, along), out_shape=ja...]
  transfers between devices with their start and end apart: 1 -> 0, of which waited for: 1 -> 0; matrix products, arithmetic and copies ran while one was open for 0% -> 0% of each run, Pallas kernels for 0% -> 0%
where the time goes in v2:
time: 55.1 us; the launch traced here: 54.8 us
  Pallas kernels  51.5 us (93%)
  matrix products  2.63 us (5%)
  other arithmetic  0.67 us (1%)
    pallas_call x1, Pallas kernels, sum_everywhere(): pl.pallas_call(functools.partial(sum_kernel, across, along), out_shape=ja...  31.4 us
    pallas_call x1, Pallas kernels, partial_spectrum(): pl.pallas_call(functools.partial(partial_kernel, group, rows), grid=(pixe...  20.1 us
    dot_general x1, matrix products, on_device(): right = dot('pxq,tqy->tpxy', mid, inverse_y)  1.36 us
    dot_general x1, matrix products, on_device(): left = dot('tkx,pkq->tpxq', inverse_x, total)  1.27 us

profile of v2, /device:TPU:0, one launch (start us, length us, event | category | flops | bytes accessed | tf_op | source)
XLA Modules:
  0.0 54.8 jit_solution(3691242027671894548)
XLA Ops:
  0.0 20.1 %partial_spectrum.1 = f32[2,256,256]{2,1,0:T(8,128)} custom-call(s32[2,32]{1,0:T(2,128)} %coords.1, f32[4]{0:T(128)} %aber.1, bf16[2048,512]{1,0:T(8,128)(2,1)} %bitcast.41, bf16[512,512]{1,0:T(8,128)(2,1)} %constant.24.clone.forward, bf16[8,256,128]{2,1,0:T(8,128)(2,1)} %constant.25.clone.columns), custom_call_target="tpu_custom_call" | custom-call | tf_op jit(solution)/shard_map/partial_spectrum/pallas_call | solution.py:245
  20.1 31.4 %sum_everywhere.1 = bf16[8,4,16,256]{3,2,1,0:T(8,128)(2,1)} custom-call(f32[8,64,256]{2,1,0:T(8,128)} %bitcast.42), custom_call_target="tpu_custom_call" | custom-call | tf_op jit(solution)/shard_map/sum_everywhere/pallas_call | solution.py:206
  51.5 1.3 %convolution_bitcast_fusion = f32[2,2,64,256]{3,2,0,1:T(8,128)S(1)} fusion(bf16[2,256,256,1]{2,1,3,0:T(8,128)(2,1)} %bitcast.43, f32[2,256,512]{1,2,0:T(8,128)} %constant.26.clone, s32[]{:T(128)S(6)} %select_n.7), kind=kOutput, calls=%fused_computation | convolution fusion | flops 201326592 | bytes 655364 | tf_op jit(solution)/shard_map/tkx,pkq->tpxq/dot_general | solution.py:286
  52.8 1.4 %convolution_bitcast_fusion.1 = f32[2,2,64,128]{3,2,1,0:T(8,128)S(1)} fusion(f32[2,256,512]{1,2,0:T(8,128)} %constant.26.clone, s32[]{:T(128)S(6)} %select_n.6, f32[1,64,256]{2,1,0:T(8,128)S(1)} %fusion.6, f32[1,64,256]{2,1,0:T(8,128)S(1)} %fusion.8), kind=kOutput, calls=%fused_computation.1 | convolution fusion | flops 100696064 | bytes 524292 | tf_op jit(solution)/shard_map/pxq,tqy->tpxy/dot_general | solution.py:290
  54.2 0.6 %maximum_multiply_fusion = f32[2,64,128]{2,1,0:T(8,128)} fusion(f32[1,64,128]{2,1,0:T(8,128)S(1)} %get-tuple-element.6, f32[1,64,128]{2,1,0:T(8,128)S(1)} %get-tuple-element.5), kind=kLoop, calls=%fused_computation.15 | loop fusion | flops 32768 | bytes 131072 | tf_op jit(solution)/shard_map/mul | solution.py:292
  (3 shorter events, 0.0 us)

commit v3 on v2

--- a/solution.py
+++ b/solution.py
@@ -119,14 +119,14 @@
         final[...] = out[...].astype(final.dtype)
 
 
-def sum_kernel(across, along, part, total, arrived, held, crossed, own, block, *sems):
+def sum_kernel(along, across, part, total, arrived, held, crossed, own, block, *sems):
+    pix_me = lax.axis_index("pix")
     scan_me = lax.axis_index("scan")
-    pix_me = lax.axis_index("pix")
 
     def peer(axis, k):
-        if axis == "scan":
-            return lax.rem(scan_me + k, along)
-        return lax.rem(pix_me + k, across)
+        if axis == "pix":
+            return lax.rem(pix_me + k, across)
+        return lax.rem(scan_me + k, along)
 
     def copy(axis, k, source, target, stage):
         return pltpu.make_async_remote_copy(
@@ -139,7 +139,7 @@
         )
 
     barrier = pltpu.get_barrier_semaphore()
-    for axis, count in (("scan", along), ("pix", across)):
+    for axis, count in (("pix", across), ("scan", along)):
         for k in range(1, count):
             pl.semaphore_signal(
                 barrier,
@@ -147,46 +147,46 @@
                 device_id={axis: peer(axis, k)},
                 device_id_type=pl.DeviceIdType.MESH,
             )
-    pl.semaphore_wait(barrier, along + across - 2)
+    pl.semaphore_wait(barrier, across + along - 2)
 
     pending = [
-        copy("scan", k, part.at[peer("scan", k)], arrived.at[k], 0) for k in range(1, along)
+        copy("pix", k, part.at[peer("pix", k)], arrived.at[k], 0) for k in range(1, across)
     ]
     for c in pending:
         c.start()
     for c in pending:
         c.wait_recv()
     lines = own.shape[0]
-    for j in range(across):
+    for j in range(along):
         rows = pl.ds(j * lines, lines)
-        summed = part[scan_me, rows, :].astype(jnp.float32)
-        for k in range(1, along):
+        summed = part[pix_me, rows, :].astype(jnp.float32)
+        for k in range(1, across):
             summed += arrived[k, rows, :].astype(jnp.float32)
         held[j] = summed.astype(held.dtype)
 
     second = [
-        copy("pix", k, held.at[peer("pix", k)], crossed.at[k], 1) for k in range(1, across)
+        copy("scan", k, held.at[peer("scan", k)], crossed.at[k], 1) for k in range(1, along)
     ]
     for c in second:
         c.start()
     for c in second:
         c.wait_recv()
-    summed = held[pix_me].astype(jnp.float32)
-    for k in range(1, across):
+    summed = held[scan_me].astype(jnp.float32)
+    for k in range(1, along):
         summed += crossed[k].astype(jnp.float32)
     own[...] = summed.astype(own.dtype)
-    block[pix_me] = own[...]
-
-    third = [copy("pix", k, own, block.at[pix_me], 2) for k in range(1, across)]
+    block[scan_me] = own[...]
+
+    third = [copy("scan", k, own, block.at[scan_me], 2) for k in range(1, along)]
     for c in third:
         c.start()
     for c in third:
         c.wait_recv()
 
-    fourth = [copy("scan", k, block, total.at[scan_me], 3) for k in range(1, along)]
+    fourth = [copy("pix", k, block, total.at[pix_me], 3) for k in range(1, across)]
     for c in fourth:
         c.start()
-    total[scan_me] = block[...]
+    total[pix_me] = block[...]
     for c in fourth:
         c.wait_recv()
     for c in pending + second + third + fourth:
@@ -194,29 +194,29 @@
 
 
 def sum_everywhere(partial):
+    across = lax.axis_size("pix")
     along = lax.axis_size("scan")
-    across = lax.axis_size("pix")
     parts, band_x, band_y = partial.shape
-    lines = parts * band_x // (along * across)
-    if parts * band_x % (16 * along * across):
-        return lax.psum(partial.astype(jnp.float32), ("pix", "scan"))
+    lines = parts * band_x // (across * along)
+    if parts * band_x % (16 * across * along):
+        return lax.psum(partial.astype(jnp.float32), ("scan", "pix"))
     narrow = jnp.bfloat16
-    pieces = (along, across * lines, band_y)
+    pieces = (across, along * lines, band_y)
     vmem = pl.BlockSpec(memory_space=pltpu.VMEM)
     total = pl.pallas_call(
-        functools.partial(sum_kernel, across, along),
-        out_shape=jax.ShapeDtypeStruct((along, across, lines, band_y), narrow),
+        functools.partial(sum_kernel, along, across),
+        out_shape=jax.ShapeDtypeStruct((across, along, lines, band_y), narrow),
         in_specs=[vmem],
         out_specs=vmem,
         scratch_shapes=[
             pltpu.VMEM(pieces, partial.dtype),
-            pltpu.VMEM((across, lines, band_y), narrow),
-            pltpu.VMEM((across, lines, band_y), narrow),
+            pltpu.VMEM((along, lines, band_y), jnp.float32),
+            pltpu.VMEM((along, lines, band_y), jnp.float32),
             pltpu.VMEM((lines, band_y), narrow),
-            pltpu.VMEM((across, lines, band_y), narrow),
+            pltpu.VMEM((along, lines, band_y), narrow),
         ]
-        + [pltpu.SemaphoreType.DMA((c,)) for c in (along, along, across, across)]
-        + [pltpu.SemaphoreType.DMA((c,)) for c in (across, across, along, along)],
+        + [pltpu.SemaphoreType.DMA((c,)) for c in (across, across, along, along)]
+        + [pltpu.SemaphoreType.DMA((c,)) for c in (along, along, across, across)],
         compiler_params=pltpu.CompilerParams(collective_id=0, has_side_effects=True),
         name="sum_everywhere",
     )(partial.reshape(pieces))
@@ -245,7 +245,7 @@
     return pl.pallas_call(
         functools.partial(partial_kernel, group, rows),
         grid=(pixels // group,),
-        out_shape=jax.ShapeDtypeStruct((2, band_x, band_y), jnp.float32),
+        out_shape=jax.ShapeDtypeStruct((2, band_x, band_y), jnp.bfloat16),
         in_specs=[
             pl.BlockSpec(memory_space=pltpu.SMEM),
             pl.BlockSpec(memory_space=pltpu.SMEM),

time: 55.1 us -> 48.5 us (0.88)
  Pallas kernels: 51.5 us -> 44.8 us
    pallas_call x1, Pallas kernels: 31.4 us -> 24.8 us  [sum_everywhere(): pl.pallas_call(functools.partial(sum_kernel, along, across), out_shape=ja...]
where the time goes in v3:
time: 48.5 us; the launch traced here: 48.2 us
  Pallas kernels  44.8 us (92%)
  matrix products  2.63 us (5%)
  other arithmetic  0.67 us (1%)
    pallas_call x1, Pallas kernels, sum_everywhere(): pl.pallas_call(functools.partial(sum_kernel, along, across), out_shape=ja...  24.8 us
    pallas_call x1, Pallas kernels, partial_spectrum(): pl.pallas_call(functools.partial(partial_kernel, group, rows), grid=(pixe...  20.1 us
    dot_general x1, matrix products, on_device(): right = dot('pxq,tqy->tpxy', mid, inverse_y)  1.36 us
    dot_general x1, matrix products, on_device(): left = dot('tkx,pkq->tpxq', inverse_x, total)  1.27 us

profile of v3, /device:TPU:0, one launch (start us, length us, event | category | flops | bytes accessed | tf_op | source)
XLA Modules:
  0.0 48.2 jit_solution(6805557385154548926)
XLA Ops:
  0.0 20.1 %partial_spectrum.1 = bf16[2,256,256]{2,1,0:T(8,128)(2,1)} custom-call(s32[2,32]{1,0:T(2,128)} %coords.1, f32[4]{0:T(128)} %aber.1, bf16[2048,512]{1,0:T(8,128)(2,1)} %bitcast.41, bf16[512,512]{1,0:T(8,128)(2,1)} %constant.24.clone.forward, bf16[8,256,128]{2,1,0:T(8,128)(2,1)} %constant.25.clone.columns), custom_call_target="tpu_custom_call" | custom-call | tf_op jit(solution)/shard_map/partial_spectrum/pallas_call | solution.py:245
  20.1 24.8 %sum_everywhere.1 = bf16[4,8,16,256]{3,2,1,0:T(8,128)(2,1)} custom-call(bf16[4,128,256]{2,1,0:T(8,128)(2,1)} %bitcast.43), custom_call_target="tpu_custom_call" | custom-call | tf_op jit(solution)/shard_map/sum_everywhere/pallas_call | solution.py:206
  44.9 1.3 %convolution_bitcast_fusion = f32[2,2,64,256]{3,2,0,1:T(8,128)S(1)} fusion(bf16[2,256,256,1]{2,1,3,0:T(8,128)(2,1)} %bitcast.42, f32[2,256,512]{1,2,0:T(8,128)} %constant.26.clone, s32[]{:T(128)S(6)} %select_n.7), kind=kOutput, calls=%fused_computation | convolution fusion | flops 201326592 | bytes 655364 | tf_op jit(solution)/shard_map/tkx,pkq->tpxq/dot_general | solution.py:286
  46.2 1.4 %convolution_bitcast_fusion.1 = f32[2,2,64,128]{3,2,1,0:T(8,128)S(1)} fusion(f32[2,256,512]{1,2,0:T(8,128)} %constant.26.clone, s32[]{:T(128)S(6)} %select_n.6, f32[1,64,256]{2,1,0:T(8,128)S(1)} %fusion.6, f32[1,64,256]{2,1,0:T(8,128)S(1)} %fusion.8), kind=kOutput, calls=%fused_computation.1 | convolution fusion | flops 100696064 | bytes 524292 | tf_op jit(solution)/shard_map/pxq,tqy->tpxy/dot_general | solution.py:290
  47.6 0.6 %maximum_multiply_fusion = f32[2,64,128]{2,1,0:T(8,128)} fusion(f32[1,64,128]{2,1,0:T(8,128)S(1)} %get-tuple-element.6, f32[1,64,128]{2,1,0:T(8,128)S(1)} %get-tuple-element.5), kind=kLoop, calls=%fused_computation.15 | loop fusion | flops 32768 | bytes 131072 | tf_op jit(solution)/shard_map/mul | solution.py:292
  (3 shorter events, 0.0 us)

commit v4 on v3

--- a/solution.py
+++ b/solution.py
@@ -13,6 +13,7 @@
 EXTENT = 6
 REACH = STEP * EXTENT
 APERTURE = 40 * STEP * STEP
+LIMIT = math.isqrt(APERTURE)
 
 
 def centred(length):
@@ -53,19 +54,30 @@
         @pl.loop(0, tall // chunk)
         def _(i):
             at = pl.ds(pl.multiple_of(i * chunk, chunk), chunk)
-            px = lax.broadcasted_iota(jnp.int32, (chunk, wide), 0) + (
-                i * chunk - band_x // 2 - REACH
-            )
-            py = lax.broadcasted_iota(jnp.int32, (chunk, wide), 1) - (band_y // 2 + REACH)
-            inside = px * px + py * py <= APERTURE
-            phase = aberration(px, py, coeffs)
-            real = jnp.cos(phase)
-            real = jnp.where(real == 0.0, 1e-12, real)
-            base_re[at, :] = jnp.where(inside, real, 0.0)
-            base_im[at, :] = jnp.where(inside, jnp.sin(phase), 0.0)
-            for s in range(shifts):
-                tab_re[s, at, :] = base_re[at, STEP * s : STEP * s + band_y]
-                tab_im[s, at, :] = base_im[at, STEP * s : STEP * s + band_y]
+            first = i * chunk - band_x // 2 - REACH
+            near = jnp.logical_and(first <= LIMIT, first + chunk > -LIMIT)
+
+            @pl.when(jnp.logical_not(near))
+            def _():
+                for s in range(shifts):
+                    tab_re[s, at, :] = jnp.zeros((chunk, band_y), jnp.float32)
+                    tab_im[s, at, :] = jnp.zeros((chunk, band_y), jnp.float32)
+
+            @pl.when(near)
+            def _():
+                px = lax.broadcasted_iota(jnp.int32, (chunk, wide), 0) + (
+                    i * chunk - band_x // 2 - REACH
+                )
+                py = lax.broadcasted_iota(jnp.int32, (chunk, wide), 1) - (band_y // 2 + REACH)
+                inside = px * px + py * py <= APERTURE
+                phase = aberration(px, py, coeffs)
+                real = jnp.cos(phase)
+                real = jnp.where(real == 0.0, 1e-12, real)
+                base_re[at, :] = jnp.where(inside, real, 0.0)
+                base_im[at, :] = jnp.where(inside, jnp.sin(phase), 0.0)
+                for s in range(shifts):
+                    tab_re[s, at, :] = base_re[at, STEP * s : STEP * s + band_y]
+                    tab_im[s, at, :] = base_im[at, STEP * s : STEP * s + band_y]
 
     me = lax.axis_index("scan")
     table = columns[me]
@@ -276,20 +288,17 @@
     partial = partial_spectrum(scan_data, pixel_coords, aberrations, scan_count)
     total = sum_everywhere(partial)
     share = breadth // pix_count
+    scale = 1.0 / (height * breadth)
     ic, isn = table_pair(centred(height), np.arange(height), height)
-    inverse_x = jnp.asarray(np.stack([ic, isn]), jnp.float32)
-    inverse_x = lax.dynamic_slice_in_dim(inverse_x, lax.axis_index("scan") * rows, rows, 2)
+    inverse_x = jnp.asarray(np.stack([np.stack([ic, -isn]), np.stack([isn, ic])]), jnp.float32)
+    inverse_x = lax.dynamic_slice_in_dim(inverse_x, lax.axis_index("scan") * rows, rows, 3)
     jc, js = table_pair(centred(breadth), np.arange(breadth), breadth)
-    inverse_y = jnp.asarray(np.stack([jc, js]), jnp.float32)
-    inverse_y = lax.dynamic_slice_in_dim(inverse_y, lax.axis_index("pix") * share, share, 2)
+    inverse_y = np.stack([np.stack([jc, -js]), np.stack([js, jc])])
+    inverse_y = jnp.asarray(inverse_y * scale, jnp.float32)
+    inverse_y = lax.dynamic_slice_in_dim(inverse_y, lax.axis_index("pix") * share, share, 3)
     dot = functools.partial(jnp.einsum, precision=highest)
-    left = dot("tkx,pkq->tpxq", inverse_x, total)
-    mid_re = left[0, 0] - left[1, 1]
-    mid_im = left[1, 0] + left[0, 1]
-    mid = jnp.stack([mid_re, mid_im])
-    right = dot("pxq,tqy->tpxy", mid, inverse_y)
-    result = jnp.stack([right[0, 0] - right[1, 1], right[1, 0] + right[0, 1]])
-    return result * (1.0 / (height * breadth))
+    middle = dot("tpkx,pkq->txq", inverse_x, total)
+    return dot("pxq,tpqy->txy", middle, inverse_y)
 
 
 def solution(mesh):

time: 48.5 us -> 45.1 us (0.930)
  Pallas kernels: 44.8 us -> 40.8 us
  matrix products: 2.63 us -> 3.98 us
  other arithmetic: 0.67 us -> 0 us
    pallas_call x1, Pallas kernels: 20.1 us -> 16 us  [partial_spectrum(): pl.pallas_call(functools.partial(partial_kernel, group, rows), grid=(pixe...]
    dot_general x2, matrix products: 2.63 us -> 3.98 us  [the longest x1 2.11 us: on_device(): return dot('pxq,tpqy->txy', middle, inverse_y)]
    mul x1 -> x0, other arithmetic: 0.64 us -> none  [on_device(): return result * (1.0 / (height * breadth))]
where the time goes in v4:
time: 45.1 us; the launch traced here: 44.8 us
  Pallas kernels  40.8 us (90%)
  matrix products  3.98 us (9%)
    pallas_call x1, Pallas kernels, sum_everywhere(): pl.pallas_call(functools.partial(sum_kernel, along, across), out_shape=ja...  24.8 us
    pallas_call x1, Pallas kernels, partial_spectrum(): pl.pallas_call(functools.partial(partial_kernel, group, rows), grid=(pixe...  16 us
    dot_general x1, matrix products, on_device(): return dot('pxq,tpqy->txy', middle, inverse_y)  2.11 us
    dot_general x1, matrix products, on_device(): middle = dot('tpkx,pkq->txq', inverse_x, total)  1.87 us

profile of v4, /device:TPU:0, one launch (start us, length us, event | category | flops | bytes accessed | tf_op | source)
XLA Modules:
  0.0 44.8 jit_solution(17582275704468178990)
XLA Ops:
  0.0 16.0 %partial_spectrum.1 = bf16[2,256,256]{2,1,0:T(8,128)(2,1)} custom-call(s32[2,32]{1,0:T(2,128)} %coords.1, f32[4]{0:T(128)} %aber.1, bf16[2048,512]{1,0:T(8,128)(2,1)} %bitcast.16, bf16[512,512]{1,0:T(8,128)(2,1)} %constant.24.clone.forward, bf16[8,256,128]{2,1,0:T(8,128)(2,1)} %constant.25.clone.columns), custom_call_target="tpu_custom_call" | custom-call | tf_op jit(solution)/shard_map/partial_spectrum/pallas_call | solution.py:257
  16.0 24.8 %sum_everywhere.1 = bf16[4,8,16,256]{3,2,1,0:T(8,128)(2,1)} custom-call(bf16[4,128,256]{2,1,0:T(8,128)(2,1)} %bitcast.18), custom_call_target="tpu_custom_call" | custom-call | tf_op jit(solution)/shard_map/sum_everywhere/pallas_call | solution.py:218
  40.8 1.9 %convolution_bitcast_fusion = f32[2,64,256,1]{2,1,0,3:T(8,128)S(1)} fusion(bf16[2,256,256,1]{2,1,0,3:T(8,128)(2,1)} %bitcast.17, f32[2,2,256,512]{3,2,1,0:T(8,128)} %constant.26.clone, s32[]{:T(128)S(6)} %select_n.7), kind=kOutput, calls=%fused_computation | convolution fusion | flops 201326592 | bytes 917508 | tf_op jit(solution)/shard_map/tpkx,pkq->txq/dot_general | solution.py:300
  42.7 2.1 %convolution_bitcast_fusion.1 = f32[2,64,128]{2,1,0:T(8,128)} fusion(f32[2,64,256,1]{2,1,0,3:T(8,128)S(1)} %convolution_bitcast_fusion, f32[2,2,256,512]{3,2,1,0:T(8,128)} %constant.27.clone, s32[]{:T(128)S(6)} %select_n.6), kind=kOutput, calls=%fused_computation.1 | convolution fusion | flops 100663296 | bytes 720900 | tf_op jit(solution)/shard_map/pxq,tpqy->txy/dot_general | solution.py:301

commit v5 on v4

--- a/solution.py
+++ b/solution.py
@@ -50,6 +50,7 @@
         out[...] = jnp.zeros_like(out)
         tall, wide = base_re.shape
         chunk = 16
+        used = min(wide, -(-(band_y // 2 + REACH + LIMIT + 1) // 128) * 128)
 
         @pl.loop(0, tall // chunk)
         def _(i):
@@ -65,16 +66,19 @@
 
             @pl.when(near)
             def _():
-                px = lax.broadcasted_iota(jnp.int32, (chunk, wide), 0) + (
+                px = lax.broadcasted_iota(jnp.int32, (chunk, used), 0) + (
                     i * chunk - band_x // 2 - REACH
                 )
-                py = lax.broadcasted_iota(jnp.int32, (chunk, wide), 1) - (band_y // 2 + REACH)
+                py = lax.broadcasted_iota(jnp.int32, (chunk, used), 1) - (band_y // 2 + REACH)
                 inside = px * px + py * py <= APERTURE
                 phase = aberration(px, py, coeffs)
                 real = jnp.cos(phase)
                 real = jnp.where(real == 0.0, 1e-12, real)
-                base_re[at, :] = jnp.where(inside, real, 0.0)
-                base_im[at, :] = jnp.where(inside, jnp.sin(phase), 0.0)
+                base_re[at, :used] = jnp.where(inside, real, 0.0)
+                base_im[at, :used] = jnp.where(inside, jnp.sin(phase), 0.0)
+                if used < wide:
+                    base_re[at, used:] = jnp.zeros((chunk, wide - used), jnp.float32)
+                    base_im[at, used:] = jnp.zeros((chunk, wide - used), jnp.float32)
                 for s in range(shifts):
                     tab_re[s, at, :] = base_re[at, STEP * s : STEP * s + band_y]
                     tab_im[s, at, :] = base_im[at, STEP * s : STEP * s + band_y]
@@ -288,17 +292,20 @@
     partial = partial_spectrum(scan_data, pixel_coords, aberrations, scan_count)
     total = sum_everywhere(partial)
     share = breadth // pix_count
-    scale = 1.0 / (height * breadth)
     ic, isn = table_pair(centred(height), np.arange(height), height)
-    inverse_x = jnp.asarray(np.stack([np.stack([ic, -isn]), np.stack([isn, ic])]), jnp.float32)
-    inverse_x = lax.dynamic_slice_in_dim(inverse_x, lax.axis_index("scan") * rows, rows, 3)
+    inverse_x = jnp.asarray(np.stack([ic, isn]), jnp.float32)
+    inverse_x = lax.dynamic_slice_in_dim(inverse_x, lax.axis_index("scan") * rows, rows, 2)
     jc, js = table_pair(centred(breadth), np.arange(breadth), breadth)
-    inverse_y = np.stack([np.stack([jc, -js]), np.stack([js, jc])])
-    inverse_y = jnp.asarray(inverse_y * scale, jnp.float32)
-    inverse_y = lax.dynamic_slice_in_dim(inverse_y, lax.axis_index("pix") * share, share, 3)
+    inverse_y = jnp.asarray(np.stack([jc, js]) * (1.0 / (height * breadth)), jnp.float32)
+    inverse_y = lax.dynamic_slice_in_dim(inverse_y, lax.axis_index("pix") * share, share, 2)
     dot = functools.partial(jnp.einsum, precision=highest)
-    middle = dot("tpkx,pkq->txq", inverse_x, total)
-    return dot("pxq,tpqy->txy", middle, inverse_y)
+    left = dot("tkx,pkq->tpxq", inverse_x, total)
+    mid_re = left[0, 0] - left[1, 1]
+    mid_im = left[1, 0] + left[0, 1]
+    mid = jnp.stack([mid_re, mid_im])
+    right = dot("pxq,tqy->tpxy", mid, inverse_y)
+    result = jnp.stack([right[0, 0] - right[1, 1], right[1, 0] + right[0, 1]])
+    return result
 
 
 def solution(mesh):

time: 45.1 us -> 43.7 us (0.969)
  matrix products: 3.98 us -> 2.53 us
  other arithmetic: 0 us -> 0.67 us
  Pallas kernels: 40.8 us -> 40.2 us
    dot_general x2, matrix products: 3.98 us -> 2.53 us  [the longest x1 1.27 us: on_device(): left = dot('tkx,pkq->tpxq', inverse_x, total)]
    another operation x0 -> x1, other arithmetic: none -> 0.64 us  [on_device(): result = jnp.stack([right[0, 0] - right[1, 1], right[1, 0] + right[0, 1]])]
    pallas_call x1, Pallas kernels: 16 us -> 15.4 us  [partial_spectrum(): pl.pallas_call(functools.partial(partial_kernel, group, rows), grid=(pixe...]
where the time goes in v5:
time: 43.7 us; the launch traced here: 43.5 us
  Pallas kernels  40.2 us (92%)
  matrix products  2.53 us (6%)
  other arithmetic  0.67 us (2%)
    pallas_call x1, Pallas kernels, sum_everywhere(): pl.pallas_call(functools.partial(sum_kernel, along, across), out_shape=ja...  24.8 us
    pallas_call x1, Pallas kernels, partial_spectrum(): pl.pallas_call(functools.partial(partial_kernel, group, rows), grid=(pixe...  15.4 us
    dot_general x1, matrix products, on_device(): left = dot('tkx,pkq->tpxq', inverse_x, total)  1.27 us
    dot_general x1, matrix products, on_device(): right = dot('pxq,tqy->tpxy', mid, inverse_y)  1.26 us

profile of v5, /device:TPU:0, one launch (start us, length us, event | category | flops | bytes accessed | tf_op | source)
XLA Modules:
  0.0 43.5 jit_solution(18408346525104934363)
XLA Ops:
  0.0 15.4 %partial_spectrum.1 = bf16[2,256,256]{2,1,0:T(8,128)(2,1)} custom-call(s32[2,32]{1,0:T(2,128)} %coords.1, f32[4]{0:T(128)} %aber.1, bf16[2048,512]{1,0:T(8,128)(2,1)} %bitcast.41, bf16[512,512]{1,0:T(8,128)(2,1)} %constant.24.clone.forward, bf16[8,256,128]{2,1,0:T(8,128)(2,1)} %constant.25.clone.columns), custom_call_target="tpu_custom_call" | custom-call | tf_op jit(solution)/shard_map/partial_spectrum/pallas_call | solution.py:261
  15.4 24.8 %sum_everywhere.1 = bf16[4,8,16,256]{3,2,1,0:T(8,128)(2,1)} custom-call(bf16[4,128,256]{2,1,0:T(8,128)(2,1)} %bitcast.43), custom_call_target="tpu_custom_call" | custom-call | tf_op jit(solution)/shard_map/sum_everywhere/pallas_call | solution.py:222
  40.2 1.3 %convolution_bitcast_fusion = f32[2,2,64,256]{3,2,0,1:T(8,128)S(1)} fusion(bf16[2,256,256,1]{2,1,3,0:T(8,128)(2,1)} %bitcast.42, f32[2,256,512]{1,2,0:T(8,128)} %constant.26.clone, s32[]{:T(128)S(6)} %select_n.7), kind=kOutput, calls=%fused_computation | convolution fusion | flops 201326592 | bytes 655364 | tf_op jit(solution)/shard_map/tkx,pkq->tpxq/dot_general | solution.py:302
  41.5 1.3 %convolution_bitcast_fusion.1 = f32[2,2,64,128]{3,2,1,0:T(8,128)S(1)} fusion(f32[2,256,512]{2,1,0:T(8,128)} %constant.27.clone, s32[]{:T(128)S(6)} %select_n.6, f32[1,64,256]{2,1,0:T(8,128)S(1)} %fusion.6, f32[1,64,256]{2,1,0:T(8,128)S(1)} %fusion.8), kind=kOutput, calls=%fused_computation.1 | convolution fusion | flops 100696064 | bytes 524292 | tf_op jit(solution)/shard_map/pxq,tqy->tpxy/dot_general | solution.py:306
  42.8 0.6 %pad_maximum_fusion = f32[2,64,128]{2,1,0:T(8,128)} fusion(f32[1,64,128]{2,1,0:T(8,128)S(1)} %get-tuple-element.6, f32[1,64,128]{2,1,0:T(8,128)S(1)} %get-tuple-element.5), kind=kLoop, calls=%fused_computation.15 | loop fusion | flops 16384 | bytes 131072 | tf_op jit(solution)/shard_map/stack | solution.py:307
  (3 shorter events, 0.0 us)
